TPU v7x, 32 devices: a whole 2x2x4 slice. The times are simulated.
32 devices in a mesh: seq: 4 (over z), tok: 8 (over y, x, core).
Axes of the slice: x: 2, y: 2, z: 4, core: 2. Of those that a mesh axis runs over, the one named last changes fastest.
Arguments:
- tokens: bfloat16 [4, 4, 2048, 768], P(None, 'seq', 'tok'), may hold values from -6 to 6
- cotangent: bfloat16 [4, 4, 2048, 768], P(None, 'seq', 'tok'), may hold values from -6 to 6
- documents: int32 [4, 4, 2048], P(None, 'seq', 'tok'), may hold values from 0 to 7, never falling along the last dimension, each value on 1 to 1536 neighbouring positions
- positions: int32 [4, 4, 16], P(None, 'seq', 'tok'), may hold values from 0 to 63
- inner_mixing: bfloat16 [768, 2304], P(('seq', 'tok')), may hold values from -0.21875 to 0.21875
- inner_output: bfloat16 [768, 768], P(('seq', 'tok')), may hold values from -0.875 to 0.875
- inner_expand: bfloat16 [768, 3072], P(('seq', 'tok')), may hold values from -0.21875 to 0.21875
- inner_shrink: bfloat16 [3072, 768], P(('seq', 'tok')), may hold values from -0.15625 to 0.15625
- inner_lift: bfloat16 [3072], P(('seq', 'tok')), may hold values from -3 to 3
- inner_shifts: bfloat16 [6, 768], P(None, ('seq', 'tok')), may hold values from -3 to 3
- inner_gains: bfloat16 [2, 768], P(None, ('seq', 'tok')), may hold values from 0.5 to 1.5
- outer_mixing: bfloat16 [768, 2304], P(('seq', 'tok')), may hold values from -0.21875 to 0.21875
- outer_output: bfloat16 [768, 768], P(('seq', 'tok')), may hold values from -0.875 to 0.875
- outer_expand: bfloat16 [768, 3072], P(('seq', 'tok')), may hold values from -0.21875 to 0.21875
- outer_shrink: bfloat16 [3072, 768], P(('seq', 'tok')), may hold values from -0.15625 to 0.15625
- outer_lift: bfloat16 [3072], P(('seq', 'tok')), may hold values from -3 to 3
- outer_shifts: bfloat16 [6, 768], P(None, ('seq', 'tok')), may hold values from -3 to 3
- outer_gains: bfloat16 [2, 768], P(None, ('seq', 'tok')), may hold values from 0.5 to 1.5
- position_table: bfloat16 [64, 768], P(None, ('seq', 'tok')), may hold values from -5 to 5
Outputs:
- output: bfloat16 [4, 4, 2048, 768], P(None, 'seq', 'tok')
- tokens_gradient: bfloat16 [4, 4, 2048, 768], P(None, 'seq', 'tok')
- inner_mixing_gradient: float32 [768, 2304], P(('seq', 'tok'))
- inner_output_gradient: float32 [768, 768], P(('seq', 'tok'))
- inner_expand_gradient: float32 [768, 3072], P(('seq', 'tok'))
- inner_shrink_gradient: float32 [3072, 768], P(('seq', 'tok'))
- inner_lift_gradient: float32 [3072], P(('seq', 'tok'))
- inner_shifts_gradient: float32 [6, 768], P(None, ('seq', 'tok'))
- inner_gains_gradient: float32 [2, 768], P(None, ('seq', 'tok'))
- outer_mixing_gradient: float32 [768, 2304], P(('seq', 'tok'))
- outer_output_gradient: float32 [768, 768], P(('seq', 'tok'))
- outer_expand_gradient: float32 [768, 3072], P(('seq', 'tok'))
- outer_shrink_gradient: float32 [3072, 768], P(('seq', 'tok'))
- outer_lift_gradient: float32 [3072], P(('seq', 'tok'))
- outer_shifts_gradient: float32 [6, 768], P(None, ('seq', 'tok'))
- outer_gains_gradient: float32 [2, 768], P(None, ('seq', 'tok'))
- position_table_gradient: float32 [64, 768], P(None, ('seq', 'tok'))
Inputs may be any that keep to these rules, and one draw needn't show every extreme that they name: `documents`: within each sequence the document numbers never fall along the positions; each document holds 1 to 1536 consecutive tokens and one holds exactly 1536.
All inputs are finite; a program needn't handle non-finite values.
Results may differ from a plain program's by a relative error of at most 0.028.
Values may be sent and summed in bfloat16 or wider, within the bound.
No kernel may reach another device: no remote copies, remote signals or barrier semaphores. Data moves between devices by JAX's collectives and lax.ppermute only.
A program may use at most 320 MiB of HBM per device.

v0:
```python
import jax
import jax.numpy as jnp
from jax import lax
from jax.sharding import PartitionSpec as P

H = 12
HD = 64
SEG = 128


EPS = 1e-05
NEGATIVE = -1e30
ROOT_HALF = 0.7071067811865476
INVERSE_ROOT_TAU = 0.3989422804014327


def product(left, right):
    return jnp.dot(left, right, preferred_element_type=jnp.float32)


def across(left, right):
    return lax.dot_general(
        left, right, (((0,), (0,)), ((), ())), preferred_element_type=jnp.float32
    )


def against(left, right):
    return lax.dot_general(
        left, right, (((1,), (1,)), ((), ())), preferred_element_type=jnp.float32
    )


def normalize(value, gain, shift):
    centered = value - jnp.mean(value, -1, keepdims=True)
    factor = lax.rsqrt(jnp.mean(centered * centered, -1, keepdims=True) + EPS)
    unit = centered * factor
    return (unit * gain + shift, (unit, factor))


def normalize_back(delta, gain, saved):
    unit, factor = saved
    scaled = delta * gain
    moved = (
        scaled
        - jnp.mean(scaled, -1, keepdims=True)
        - unit * jnp.mean(scaled * unit, -1, keepdims=True)
    )
    return (moved * factor, jnp.sum(delta * unit, 0), jnp.sum(delta, 0))


def gelu_slope(value):
    return (
        0.5 * (1.0 + lax.erf(value * ROOT_HALF))
        + value * jnp.exp(-0.5 * value * value) * INVERSE_ROOT_TAU
    )


def attend_forward(query, key, value, allowed):
    scores = jnp.where(
        allowed,
        jnp.einsum("aqhd,akhd->ahqk", query, key, preferred_element_type=jnp.float32),
        NEGATIVE,
    )
    top = jnp.max(scores, -1, keepdims=True)
    spread = top + jnp.log(jnp.sum(jnp.exp(scores - top), -1, keepdims=True))
    weights = jnp.exp(scores - spread).astype(jnp.bfloat16)
    return (
        jnp.einsum("ahqk,akhd->aqhd", weights, value, preferred_element_type=jnp.float32),
        spread,
    )


def attend_backward(query, key, value, allowed, spread, delta):
    scores = jnp.where(
        allowed,
        jnp.einsum("aqhd,akhd->ahqk", query, key, preferred_element_type=jnp.float32),
        NEGATIVE,
    )
    weights = jnp.exp(scores - spread)
    pressure = jnp.einsum("aqhd,akhd->ahqk", delta, value, preferred_element_type=jnp.float32)
    score_delta = (weights * (pressure - jnp.sum(weights * pressure, -1, keepdims=True))).astype(
        jnp.bfloat16
    )
    query_delta = jnp.einsum(
        "ahqk,akhd->aqhd", score_delta, key, preferred_element_type=jnp.float32
    )
    key_delta = jnp.einsum(
        "ahqk,aqhd->akhd", score_delta, query, preferred_element_type=jnp.float32
    )
    value_delta = jnp.einsum(
        "ahqk,aqhd->akhd", weights.astype(jnp.bfloat16), delta, preferred_element_type=jnp.float32
    )
    return (query_delta, key_delta, value_delta)


def block_forward(start, parts, mixer):
    mixing, output, expand, shrink, lift, shifts, gains = parts
    shift = shifts.astype(jnp.float32)
    gain = gains.astype(jnp.float32)
    width = start.shape[1]
    first = start.astype(jnp.bfloat16)
    joined = product(first, mixing)
    query = ((joined[:, :width] + shift[0]) * HD ** (-0.5)).astype(jnp.bfloat16)
    key = joined[:, width : 2 * width].astype(jnp.bfloat16)
    value = (joined[:, 2 * width :] + shift[1]).astype(jnp.bfloat16)
    mixed, saved = mixer(query, key, value)
    mixed = mixed.astype(jnp.bfloat16)
    middle, first_norm = normalize(start + product(mixed, output) + shift[2], gain[0], shift[4])
    middle_low = middle.astype(jnp.bfloat16)
    raised = product(middle_low, expand) + lift.astype(jnp.float32)
    shaped = jax.nn.gelu(raised, approximate=False).astype(jnp.bfloat16)
    final, second_norm = normalize(middle + product(shaped, shrink) + shift[3], gain[1], shift[5])
    return (
        final,
        (
            first,
            query,
            key,
            value,
            saved,
            mixed,
            middle_low,
            first_norm,
            raised,
            shaped,
            second_norm,
        ),
    )


def block_backward(delta, cache, parts, mixer_back):
    mixing, output, expand, shrink, lift, shifts, gains = parts
    gain = gains.astype(jnp.float32)
    first, query, key, value, saved, mixed, middle_low, first_norm, raised, shaped, second_norm = (
        cache
    )
    lowered_delta, second_gain, fifth_shift = normalize_back(delta, gain[1], second_norm)
    third_shift = jnp.sum(lowered_delta, 0)
    lowered_low = lowered_delta.astype(jnp.bfloat16)
    shrink_grad = across(shaped, lowered_low)
    raised_delta = against(lowered_low, shrink) * gelu_slope(raised)
    lift_grad = jnp.sum(raised_delta, 0)
    raised_low = raised_delta.astype(jnp.bfloat16)
    expand_grad = across(middle_low, raised_low)
    middle_delta = lowered_delta + against(raised_low, expand)
    summed_delta, first_gain, fourth_shift = normalize_back(middle_delta, gain[0], first_norm)
    second_shift = jnp.sum(summed_delta, 0)
    summed_low = summed_delta.astype(jnp.bfloat16)
    output_grad = across(mixed, summed_low)
    mixed_delta = against(summed_low, output).astype(jnp.bfloat16)
    query_delta, key_delta, value_delta = mixer_back(mixed_delta, query, key, value, saved)
    query_delta = query_delta * HD ** (-0.5)
    joined = jnp.concatenate([query_delta, key_delta, value_delta], 1).astype(jnp.bfloat16)
    mixing_grad = across(first, joined)
    start_delta = summed_delta + against(joined, mixing)
    shifts_grad = jnp.stack(
        [
            jnp.sum(query_delta, 0),
            jnp.sum(value_delta, 0),
            second_shift,
            third_shift,
            fourth_shift,
            fifth_shift,
        ]
    )
    gains_grad = jnp.stack([first_gain, second_gain])
    return (
        start_delta,
        (mixing_grad, output_grad, expand_grad, shrink_grad, lift_grad, shifts_grad, gains_grad),
    )


def per_device(
    tokens,
    cotangent,
    documents,
    positions,
    inner_mixing,
    inner_output,
    inner_expand,
    inner_shrink,
    inner_lift,
    inner_shifts,
    inner_gains,
    outer_mixing,
    outer_output,
    outer_expand,
    outer_shrink,
    outer_lift,
    outer_shifts,
    outer_gains,
    position_table,
):
    batches = tokens.shape[0]
    rows = tokens.shape[2]
    width = tokens.shape[3]
    slots = rows // SEG
    slot_docs = lax.all_gather(documents[:, 0, ::SEG], "tok", axis=1, tiled=True)
    inner_kept = (
        lax.all_gather(inner_mixing, ("seq", "tok"), axis=0, tiled=True),
        lax.all_gather(inner_output, ("seq", "tok"), axis=0, tiled=True),
        lax.all_gather(inner_expand, ("seq", "tok"), axis=0, tiled=True),
        lax.all_gather(inner_shrink, ("seq", "tok"), axis=0, tiled=True),
        lax.all_gather(inner_lift, ("seq", "tok"), axis=0, tiled=True),
        lax.all_gather(inner_shifts, ("seq", "tok"), axis=1, tiled=True),
        lax.all_gather(inner_gains, ("seq", "tok"), axis=1, tiled=True),
    )
    outer_kept = (
        lax.all_gather(outer_mixing, ("seq", "tok"), axis=0, tiled=True),
        lax.all_gather(outer_output, ("seq", "tok"), axis=0, tiled=True),
        lax.all_gather(outer_expand, ("seq", "tok"), axis=0, tiled=True),
        lax.all_gather(outer_shrink, ("seq", "tok"), axis=0, tiled=True),
        lax.all_gather(outer_lift, ("seq", "tok"), axis=0, tiled=True),
        lax.all_gather(outer_shifts, ("seq", "tok"), axis=1, tiled=True),
        lax.all_gather(outer_gains, ("seq", "tok"), axis=1, tiled=True),
        lax.all_gather(position_table, ("seq", "tok"), axis=1, tiled=True),
    )
    inner_total = None
    outer_total = None
    outputs = []
    input_grads = []
    for batch in range(batches):
        docs = documents[batch, 0]
        slot_ids = docs.reshape(slots, SEG)
        within_allowed = (slot_ids[:, :, None] == slot_ids[:, None, :])[:, None]
        cross_allowed = (docs[::SEG][:, None] == slot_docs[batch][None, :])[None, None]
        shape = (slots, SEG, H, HD)
        narrow = (1, slots, H, HD)

        def within_mix(query, key, value):
            mixed, spread = attend_forward(
                query.reshape(shape), key.reshape(shape), value.reshape(shape), within_allowed
            )
            return (mixed.reshape(rows, width), spread)

        def within_back(delta, query, key, value, spread):
            deltas = attend_backward(
                query.reshape(shape),
                key.reshape(shape),
                value.reshape(shape),
                within_allowed,
                spread,
                delta.reshape(shape),
            )
            return tuple((part.reshape(rows, width) for part in deltas))

        def cross_mix(query, key, value):
            key_all, value_all = (
                lax.all_gather(key, "tok", axis=0, tiled=True),
                lax.all_gather(value, "tok", axis=0, tiled=True),
            )
            wide_shape = (1, key_all.shape[0], H, HD)
            mixed, spread = attend_forward(
                query.reshape(narrow),
                key_all.reshape(wide_shape),
                value_all.reshape(wide_shape),
                cross_allowed,
            )
            return (mixed.reshape(slots, width), (key_all, value_all, spread))

        def cross_back(delta, query, key, value, saved):
            key_all, value_all, spread = saved
            wide_shape = (1, key_all.shape[0], H, HD)
            query_delta, key_delta, value_delta = attend_backward(
                query.reshape(narrow),
                key_all.reshape(wide_shape),
                value_all.reshape(wide_shape),
                cross_allowed,
                spread,
                delta.reshape(narrow),
            )
            key_own, value_own = (
                lax.psum_scatter(
                    key_delta.reshape(-1, width), "tok", scatter_dimension=0, tiled=True
                ),
                lax.psum_scatter(
                    value_delta.reshape(-1, width), "tok", scatter_dimension=0, tiled=True
                ),
            )
            return (query_delta.reshape(slots, width), key_own, value_own)

        start = tokens[batch, 0].astype(jnp.float32)
        hidden, inner_cache = block_forward(start, inner_kept, within_mix)
        grouped = hidden.reshape(slots, SEG, width)
        table = outer_kept[7]
        picked = (
            positions[batch, 0][:, None] == jnp.arange(table.shape[0], dtype=jnp.int32)[None, :]
        ).astype(jnp.bfloat16)
        summary = grouped[:, 0] + product(picked, table)
        summary_out, outer_cache = block_forward(summary, outer_kept[:7], cross_mix)
        outputs.append(
            jnp.concatenate([summary_out[:, None], grouped[:, 1:]], 1)
            .reshape(rows, width)
            .astype(jnp.bfloat16)
        )
        incoming = cotangent[batch, 0].astype(jnp.float32).reshape(slots, SEG, width)
        summary_delta, outer_grads = block_backward(
            incoming[:, 0], outer_cache, outer_kept[:7], cross_back
        )
        table_grad = lax.dot_general(
            picked.astype(jnp.float32),
            summary_delta,
            (((0,), (0,)), ((), ())),
            precision=lax.Precision.HIGHEST,
        )
        hidden_delta = jnp.concatenate([summary_delta[:, None], incoming[:, 1:]], 1).reshape(
            rows, width
        )
        start_delta, inner_grads = block_backward(
            hidden_delta, inner_cache, inner_kept, within_back
        )
        input_grads.append(start_delta.astype(jnp.bfloat16))
        outer_grads = outer_grads + (table_grad,)
        inner_total = (
            tuple(inner_grads)
            if inner_total is None
            else tuple(jax.tree.map(jnp.add, tuple(inner_total), tuple(inner_grads)))
        )
        outer_total = (
            tuple(outer_grads)
            if outer_total is None
            else tuple(jax.tree.map(jnp.add, tuple(outer_total), tuple(outer_grads)))
        )
    inner_total = (
        lax.psum_scatter(inner_total[0], ("seq", "tok"), scatter_dimension=0, tiled=True),
        lax.psum_scatter(inner_total[1], ("seq", "tok"), scatter_dimension=0, tiled=True),
        lax.psum_scatter(inner_total[2], ("seq", "tok"), scatter_dimension=0, tiled=True),
        lax.psum_scatter(inner_total[3], ("seq", "tok"), scatter_dimension=0, tiled=True),
        lax.psum_scatter(inner_total[4], ("seq", "tok"), scatter_dimension=0, tiled=True),
        lax.psum_scatter(inner_total[5], ("seq", "tok"), scatter_dimension=1, tiled=True),
        lax.psum_scatter(inner_total[6], ("seq", "tok"), scatter_dimension=1, tiled=True),
    )
    outer_total = (
        lax.psum_scatter(outer_total[0], ("seq", "tok"), scatter_dimension=0, tiled=True),
        lax.psum_scatter(outer_total[1], ("seq", "tok"), scatter_dimension=0, tiled=True),
        lax.psum_scatter(outer_total[2], ("seq", "tok"), scatter_dimension=0, tiled=True),
        lax.psum_scatter(outer_total[3], ("seq", "tok"), scatter_dimension=0, tiled=True),
        lax.psum_scatter(outer_total[4], ("seq", "tok"), scatter_dimension=0, tiled=True),
        lax.psum_scatter(outer_total[5], ("seq", "tok"), scatter_dimension=1, tiled=True),
        lax.psum_scatter(outer_total[6], ("seq", "tok"), scatter_dimension=1, tiled=True),
        lax.psum_scatter(outer_total[7], ("seq", "tok"), scatter_dimension=1, tiled=True),
    )
    output = jnp.stack(outputs)[:, None]
    tokens_gradient = jnp.stack(input_grads)[:, None]
    return (
        output,
        tokens_gradient,
        inner_total[0],
        inner_total[1],
        inner_total[2],
        inner_total[3],
        inner_total[4],
        inner_total[5],
        inner_total[6],
        outer_total[0],
        outer_total[1],
        outer_total[2],
        outer_total[3],
        outer_total[4],
        outer_total[5],
        outer_total[6],
        outer_total[7],
    )


def solution(mesh):
    return jax.shard_map(
        per_device,
        mesh=mesh,
        in_specs=(
            P(None, "seq", "tok", None),
            P(None, "seq", "tok", None),
            P(None, "seq", "tok"),
            P(None, "seq", "tok"),
            P(("seq", "tok"), None),
            P(("seq", "tok"), None),
            P(("seq", "tok"), None),
            P(("seq", "tok"), None),
            P(("seq", "tok")),
            P(None, ("seq", "tok")),
            P(None, ("seq", "tok")),
            P(("seq", "tok"), None),
            P(("seq", "tok"), None),
            P(("seq", "tok"), None),
            P(("seq", "tok"), None),
            P(("seq", "tok")),
            P(None, ("seq", "tok")),
            P(None, ("seq", "tok")),
            P(None, ("seq", "tok")),
        ),
        out_specs=(
            P(None, "seq", "tok", None),
            P(None, "seq", "tok", None),
            P(("seq", "tok"), None),
            P(("seq", "tok"), None),
            P(("seq", "tok"), None),
            P(("seq", "tok"), None),
            P(("seq", "tok")),
            P(None, ("seq", "tok")),
            P(None, ("seq", "tok")),
            P(("seq", "tok"), None),
            P(("seq", "tok"), None),
            P(("seq", "tok"), None),
            P(("seq", "tok"), None),
            P(("seq", "tok")),
            P(None, ("seq", "tok")),
            P(None, ("seq", "tok")),
            P(None, ("seq", "tok")),
        ),
        check_vma=False,
    )
```

profile of v0, /device:TPU:0, one launch (start us, length us, event | category | flops | bytes accessed | tf_op | source)
XLA Modules:
  0.0 2130.8 jit_solution(13354472236265923134)
XLA Ops:
  23.9 43.6 %all-gather.1 = bf16[32,24,6]{1,2,0:T(8,128)(2,1)S(1)} all-gather(bf16[1,24,6]{1,2,0:T(8,128)(2,1)S(1)} %bitcast.680), channel_id=1, replica_groups=mesh['seq'=4,'tok'=8] {'seq','tok'}, dimensions={0}, use_global_device_ids=true | all-gather | bytes 9504 | tf_op jit(solution)/shard_map/all_gather | solution.py:205
  69.0 37.1 %all-reduce.19 = (bf16[3072]{0:T(1024)(128)(2,1)S(1)}, bf16[3072]{0:T(1024)(128)(2,1)S(1)}) all-reduce(bf16[3072]{0:T(1024)(128)(2,1)S(1)} %dynamic-update-slice, bf16[3072]{0:T(1024)(128)(2,1)S(1)} %dynamic-update-slice.1), channel_id=1, replica_groups=mesh['seq'=4,'tok'=8] {'seq','tok'}, use_global_device_ids=true, to_apply=%add | all-reduce | flops 6144 | bytes 24576
  107.4 39.9 %all-gather.2 = bf16[32,24,2]{1,2,0:T(2,128)(2,1)S(1)} all-gather(bf16[1,24,2]{1,2,0:T(2,128)(2,1)S(1)} %bitcast.682), channel_id=1, replica_groups=mesh['seq'=4,'tok'=8] {'seq','tok'}, dimensions={0}, use_global_device_ids=true | all-gather | bytes 3168 | tf_op jit(solution)/shard_map/all_gather | solution.py:206
  149.8 37.2 %all-gather.3 = bf16[32,24,6]{1,2,0:T(8,128)(2,1)S(1)} all-gather(bf16[1,24,6]{1,2,0:T(8,128)(2,1)S(1)} %bitcast.681), channel_id=1, replica_groups=mesh['seq'=4,'tok'=8] {'seq','tok'}, dimensions={0}, use_global_device_ids=true | all-gather | bytes 9504 | tf_op jit(solution)/shard_map/all_gather | solution.py:214
  187.9 37.8 %all-gather.6 = bf16[32,24,2]{1,2,0:T(2,128)(2,1)S(1)} all-gather(bf16[1,24,2]{1,2,0:T(2,128)(2,1)S(1)} %bitcast.683), channel_id=1, replica_groups=mesh['seq'=4,'tok'=8] {'seq','tok'}, dimensions={0}, use_global_device_ids=true | all-gather | bytes 3168 | tf_op jit(solution)/shard_map/all_gather | solution.py:215
  226.6 40.1 %all_gather.79 = bf16[64,768]{0,1:T(8,128)(2,1)} all-gather(bf16[64,24]{0,1:T(8,128)(2,1)S(1)} %copy-done.313), channel_id=1, replica_groups=mesh['seq'=4,'tok'=8] {'seq','tok'}, dimensions={1}, use_global_device_ids=true | all-gather | bytes 101376 | tf_op jit(solution)/shard_map/all_gather | solution.py:216
  335.2 11.9 fusion.2
  406.9 9.9 all-gather.5
  424.4 9.7 all-gather.7
  453.1 9.7 all-gather.9
  465.0 9.7 all-gather.10
  482.2 9.7 all-gather.11
  625.1 29.1 %all-reduce.24 = (f32[16,768]{1,0:T(8,128)}, bf16[16,768]{1,0:T(8,128)(2,1)}, f32[16,768]{1,0:T(8,128)}, bf16[16,768]{1,0:T(8,128)(2,1)}, f32[16,768]{1,0:T(8,12...) all-reduce(f32[16,768]{1,0:T(8,128)} %reshape.1283, ...), channel_id=10, replica_groups=mesh['seq'=4,'tok'=8] {'tok'}, use_global_device_ids=true, to_apply=%region_90.91.clone | all-reduce | flops 98304 | bytes 688128
  944.0 12.4 add_add_fusion.3
  970.7 14.7 add_add_fusion.2
  1042.2 56.9 %reduce-scatter.34.cloned.1.call-done = f32[64,24]{0,1:T(8,128)} async-done(((f32[64,768]{0,1:T(8,128)}), f32[64,24]{0,1:T(8,128)}) %reduce-scatter.34.cloned.1.call-update) | async-done | bytes 6160
  1099.1 104.8 %reduce-scatter.18.cloned.1.call-done = f32[24,768]{1,0:T(8,128)} async-done(((f32[768,768]{1,0:T(8,128)}), f32[24,768]{1,0:T(8,128)}) %reduce-scatter.18.cloned.1.call-update) | async-done | bytes 73744 | tf_op jit(solution)/shard_map/reduce_scatter | solution.py:326
  1203.9 103.8 %reduce-scatter.26.cloned.1.call-done = f32[24,768]{1,0:T(8,128)} async-done(((f32[768,768]{1,0:T(8,128)}), f32[24,768]{1,0:T(8,128)}) %reduce-scatter.26.cloned.1.call-update) | async-done | bytes 73744 | tf_op jit(solution)/shard_map/reduce_scatter | solution.py:335
  1307.7 125.3 %reduce-scatter.32.cloned.1.call-done = f32[24,2304]{1,0:T(8,128)} async-done(((f32[768,2304]{1,0:T(8,128)}), f32[24,2304]{1,0:T(8,128)}) %reduce-scatter.32.cloned.1.call-update) | async-done | bytes 221200
  1433.0 124.5 %reduce-scatter.24.cloned.1.call-done = f32[24,2304]{1,0:T(8,128)} async-done(((f32[768,2304]{1,0:T(8,128)}), f32[24,2304]{1,0:T(8,128)}) %reduce-scatter.24.cloned.1.call-update) | async-done | bytes 221200 | tf_op jit(solution)/shard_map/reduce_scatter | solution.py:334
  1557.5 142.2 %reduce-scatter.20.cloned.1.call-done = f32[24,3072]{1,0:T(8,128)} async-done(((f32[768,3072]{1,0:T(8,128)}), f32[24,3072]{1,0:T(8,128)}) %reduce-scatter.20.cloned.1.call-update) | async-done | bytes 294928 | tf_op jit(solution)/shard_map/reduce_scatter | solution.py:327
  1699.7 141.0 %reduce-scatter.22.cloned.1.call-done = f32[96,768]{1,0:T(8,128)} async-done(((f32[3072,768]{1,0:T(8,128)}), f32[96,768]{1,0:T(8,128)}) %reduce-scatter.22.cloned.1.call-update) | async-done | bytes 294928 | tf_op jit(solution)/shard_map/reduce_scatter | solution.py:328
  1840.7 142.0 %reduce-scatter.28.cloned.1.call-done = f32[24,3072]{1,0:T(8,128)} async-done(((f32[768,3072]{1,0:T(8,128)}), f32[24,3072]{1,0:T(8,128)}) %reduce-scatter.28.cloned.1.call-update) | async-done | bytes 294928 | tf_op jit(solution)/shard_map/reduce_scatter | solution.py:336
  1982.7 141.0 %reduce-scatter.30.cloned.1.call-done = f32[96,768]{1,0:T(8,128)} async-done(((f32[3072,768]{1,0:T(8,128)}), f32[96,768]{1,0:T(8,128)}) %reduce-scatter.30.cloned.1.call-update) | async-done | bytes 294928 | tf_op jit(solution)/shard_map/reduce_scatter | solution.py:337
  (1323 shorter events, 677.0 us)
Async XLA Ops:
  7.2 278.1 %all-gather.22.cloned.1.call-start = ((), (), s32[]{:S(2)}) async-start(), calls=%async_computation.9 | async-start | bytes 3649536 | tf_op jit(solution)/shard_map/all_gather | solution.py:200
  7.9 295.5 %all-gather.24.cloned.1.call-start = ((), (), s32[]{:S(2)}) async-start(), calls=%async_computation.10 | async-start | bytes 1216512 | tf_op jit(solution)/shard_map/all_gather | solution.py:201
  8.7 326.4 %all-gather.26.cloned.1.call-start = ((), (), s32[]{:S(2)}) async-start(), calls=%async_computation.11 | async-start | bytes 4866048 | tf_op jit(solution)/shard_map/all_gather | solution.py:202
  9.4 337.6 %all-gather.28.cloned.1.call-start = ((), (), s32[]{:S(2)}) async-start(), calls=%async_computation.12 | async-start | bytes 4866048 | tf_op jit(solution)/shard_map/all_gather | solution.py:203
  10.0 380.1 %all-gather.30.cloned.1.call-start = ((), (), s32[]{:S(2)}) async-start(), calls=%async_computation.13 | async-start | bytes 3649536 | tf_op jit(solution)/shard_map/all_gather | solution.py:209
  10.6 500.3 %all-gather.32.cloned.1.call-start = ((), (), s32[]{:S(2)}) async-start(), calls=%async_computation.14 | async-start | bytes 1216512 | tf_op jit(solution)/shard_map/all_gather | solution.py:210
  11.1 507.4 %all-gather.34.cloned.1.call-start = ((), (), s32[]{:S(2)}) async-start(), calls=%async_computation.15 | async-start | bytes 4866048 | tf_op jit(solution)/shard_map/all_gather | solution.py:211
  11.9 510.3 %all-gather.36.cloned.1.call-start = ((), (), s32[]{:S(2)}) async-start(), calls=%async_computation.16 | async-start | bytes 4866048 | tf_op jit(solution)/shard_map/all_gather | solution.py:212
  12.6 1021.7 %all-reduce.23.cloned.1.call-start = ((), (), s32[]{:S(2)}) async-start(), calls=%async_computation.26 | async-start | bytes 172032
  22.1 165.8 %copy-start.339 = (bf16[2,24]{1,0:T(2,128)(2,1)S(1)}, bf16[2,24]{1,0:T(2,128)(2,1)}, u32[]{:S(2)}) copy-start(bf16[2,24]{1,0:T(2,128)(2,1)} %param.36) | copy-start | bytes 292
  22.2 204.4 %copy-start.313 = (bf16[64,24]{0,1:T(8,128)(2,1)S(1)}, bf16[64,24]{0,1:T(8,128)(2,1)}, u32[]{:S(2)}) copy-start(bf16[64,24]{0,1:T(8,128)(2,1)} %param.37) | copy-start | bytes 9220
  22.2 244.5 %copy-start.283 = (s32[4,1,2]{0,2,1:T(2,128)S(1)}, s32[4,1,2]{0,2,1:T(2,128)}, u32[]{:S(2)}) copy-start(s32[4,1,2]{0,2,1:T(2,128)} %param.22) | copy-start | bytes 100
  22.2 261.9 %copy-start.343 = (u32[32]{0:T(128)S(1)}, u32[32]{0:T(128)}, u32[]{:S(2)}) copy-start(u32[32]{0:T(128)} %constant.199) | copy-start | bytes 388
  22.2 263.1 %copy-start.47 = (bf16[4,1,256,768]{3,2,1,0:T(8,128)(2,1)S(1)}, bf16[4,1,256,768]{3,2,1,0:T(8,128)(2,1)}, u32[]{:S(2)}) copy-start(bf16[4,1,256,768]{3,2,1,0:T(8,128)(2,1)} %param.19) | copy-start | bytes 4718596
  68.4 307.7 %copy-start.147 = (f32[768]{0:T(1024)}, f32[768]{0:T(1024)S(1)}, u32[]{:S(2)}) copy-start(f32[768]{0:T(1024)S(1)} %get-tuple-element.134) | copy-start | bytes 9220
  877.2 221.8 %reduce-scatter.34.cloned.1.call-start = ((), (), s32[]{:S(2)}) async-start(), calls=%async_computation.25 | async-start | bytes 405504
  880.3 323.6 %reduce-scatter.18.cloned.1.call-start = ((), (), s32[]{:S(2)}) async-start(), calls=%async_computation.17 | async-start | bytes 2433024 | tf_op jit(solution)/shard_map/reduce_scatter | solution.py:326
  887.7 420.1 %reduce-scatter.26.cloned.1.call-start = ((), (), s32[]{:S(2)}) async-start(), calls=%async_computation.21 | async-start | bytes 2433024 | tf_op jit(solution)/shard_map/reduce_scatter | solution.py:335
  899.7 533.3 %reduce-scatter.32.cloned.1.call-start = ((), (), s32[]{:S(2)}) async-start(), calls=%async_computation.24 | async-start | bytes 7299072
  920.9 636.6 %reduce-scatter.24.cloned.1.call-start = ((), (), s32[]{:S(2)}) async-start(), calls=%async_computation.20 | async-start | bytes 7299072 | tf_op jit(solution)/shard_map/reduce_scatter | solution.py:334
  929.4 770.4 %reduce-scatter.20.cloned.1.call-start = ((), (), s32[]{:S(2)}) async-start(), calls=%async_computation.18 | async-start | bytes 9732096 | tf_op jit(solution)/shard_map/reduce_scatter | solution.py:327
  956.4 884.3 %reduce-scatter.22.cloned.1.call-start = ((), (), s32[]{:S(2)}) async-start(), calls=%async_computation.19 | async-start | bytes 9732096 | tf_op jit(solution)/shard_map/reduce_scatter | solution.py:328
  985.4 997.3 %reduce-scatter.28.cloned.1.call-start = ((), (), s32[]{:S(2)}) async-start(), calls=%async_computation.22 | async-start | bytes 9732096 | tf_op jit(solution)/shard_map/reduce_scatter | solution.py:336
  1003.8 1119.9 %reduce-scatter.30.cloned.1.call-start = ((), (), s32[]{:S(2)}) async-start(), calls=%async_computation.23 | async-start | bytes 9732096 | tf_op jit(solution)/shard_map/reduce_scatter | solution.py:337
  (349 other events, 2006.2 us)
Sparse Core Ops, SparseCore 0:
  10.9 62.8 all-gather.21
  76.7 53.0 all-gather.23
  132.7 62.6 all-gather.25
  198.2 63.0 all-gather.27
  264.0 59.1 all-gather.29
  326.0 52.8 all-gather.31
  381.7 62.5 all-gather.33
  447.2 62.6 all-gather.35
  877.4 120.1 all-reduce.22
  1002.9 96.1 reduce-scatter.33
  1105.8 98.0 reduce-scatter.17
  1209.6 98.0 reduce-scatter.25
  1314.9 118.0 reduce-scatter.31
  1439.1 118.3 reduce-scatter.23
  1564.9 134.8 reduce-scatter.19
  1706.1 134.6 reduce-scatter.21
  1848.0 134.6 reduce-scatter.27
  1989.1 134.5 reduce-scatter.29
where the time goes:
time: 2140 us; the launch traced here: 2130 us
  waiting for transfers between devices  1090 us (51%)
  matrix products  351 us (16%)
  blocking collectives  350 us (16%)
  local copies, waits for them, and re-layouts  268 us (13%)
  other arithmetic  53.3 us (2%)
    unnamed x21, waiting for transfers between devices  187 us
    reduce_scatter x1, waiting for transfers between devices, per_device(): lax.psum_scatter(inner_total[2], ('seq', 'tok'), scatter_dimension=0, til...  142 us
    reduce_scatter x1, waiting for transfers between devices, per_device(): lax.psum_scatter(outer_total[2], ('seq', 'tok'), scatter_dimension=0, til...  142 us
    reduce_scatter x1, waiting for transfers between devices, per_device(): lax.psum_scatter(inner_total[3], ('seq', 'tok'), scatter_dimension=0, til...  141 us
    reduce_scatter x1, waiting for transfers between devices, per_device(): lax.psum_scatter(outer_total[3], ('seq', 'tok'), scatter_dimension=0, til...  141 us
    reduce_scatter x1, waiting for transfers between devices, per_device(): lax.psum_scatter(outer_total[0], ('seq', 'tok'), scatter_dimension=0, til...  125 us
    dot_general x32, matrix products, across(): lax.dot_general(left, right, (((0,), (0,)), ((), ())), preferred_element_...  118 us
    reduce_scatter x1, waiting for transfers between devices, per_device(): lax.psum_scatter(inner_total[1], ('seq', 'tok'), scatter_dimension=0, til...  105 us
  transfers between devices with their start and end apart: 18, of which 9 were waited for; matrix products, arithmetic and copies ran while one was open for 16% of the time, Pallas kernels for 0%

commit v1 on v0

v1 whole, which is shorter than its diff:
```python
import jax
import jax.numpy as jnp
from jax import lax
from jax.experimental import pallas as pl
from jax.experimental.pallas import tpu as pltpu
from jax.sharding import PartitionSpec as P

H = 12
HD = 64
SEG = 128
LANES = 128

EPS = 1e-05
NEGATIVE = -1e30
ROOT_HALF = 0.7071067811865476
INVERSE_ROOT_TAU = 0.3989422804014327
F32 = jnp.float32
BF16 = jnp.bfloat16
ALL = ("seq", "tok")


def product(left, right):
    return jnp.dot(left, right, preferred_element_type=F32)


def across(left, right):
    return lax.dot_general(left, right, (((0,), (0,)), ((), ())), preferred_element_type=F32)


def against(left, right):
    return lax.dot_general(left, right, (((1,), (1,)), ((), ())), preferred_element_type=F32)


def unit_of(value):
    centered = value - jnp.mean(value, -1, keepdims=True)
    factor = lax.rsqrt(jnp.mean(centered * centered, -1, keepdims=True) + EPS)
    return centered * factor, factor


def unit_back(delta, gain, unit, factor):
    scaled = delta * gain
    return factor * (
        scaled
        - jnp.mean(scaled, -1, keepdims=True)
        - unit * jnp.mean(scaled * unit, -1, keepdims=True)
    )


def gelu_parts(value):
    phi = 0.5 * (1.0 + lax.erf(value * ROOT_HALF))
    return value * phi, phi + value * jnp.exp(-0.5 * value * value) * INVERSE_ROOT_TAU


def two_heads(pair, low):
    zero = jnp.zeros_like(pair)
    return jnp.concatenate([jnp.where(low, pair, zero), jnp.where(low, zero, pair)], 0)


def attend_kernel(qkv_ref, col_ref, row_ref, o_ref, p_ref):
    width = o_ref.shape[1]
    low = lax.broadcasted_iota(jnp.int32, (SEG, LANES), 1) < HD
    allowed = col_ref[...] == row_ref[0]
    allowed = jnp.concatenate([allowed, allowed], 0)
    for pair in range(width // LANES):
        at = pair * LANES
        query = two_heads(qkv_ref[:, at : at + LANES], low)
        key = qkv_ref[:, width + at : width + at + LANES]
        value = qkv_ref[:, 2 * width + at : 2 * width + at + LANES]
        scores = jnp.where(allowed, against(query, key), NEGATIVE)
        weight = jnp.exp(scores - jnp.max(scores, -1, keepdims=True))
        weight = (weight / jnp.sum(weight, -1, keepdims=True)).astype(BF16)
        p_ref[0, pair] = weight
        mixed = product(weight, value)
        o_ref[:, at : at + LANES] = jnp.where(low, mixed[:SEG], mixed[SEG:]).astype(BF16)


def attend(qkv, col, row, width):
    rows = qkv.shape[0]
    segments = rows // SEG
    pairs = width // LANES
    return pl.pallas_call(
        attend_kernel,
        grid=(segments,),
        in_specs=[
            pl.BlockSpec((SEG, 3 * width), lambda i: (i, 0)),
            pl.BlockSpec((SEG, 1), lambda i: (i, 0)),
            pl.BlockSpec((1, 1, SEG), lambda i: (i, 0, 0)),
        ],
        out_specs=[
            pl.BlockSpec((SEG, width), lambda i: (i, 0)),
            pl.BlockSpec((1, pairs, 2 * SEG, SEG), lambda i: (i, 0, 0, 0)),
        ],
        out_shape=[
            jax.ShapeDtypeStruct((rows, width), BF16),
            jax.ShapeDtypeStruct((segments, pairs, 2 * SEG, SEG), BF16),
        ],
        cost_estimate=pl.CostEstimate(
            flops=8 * rows * SEG * width, bytes_accessed=rows * width * 10, transcendentals=rows * SEG * H
        ),
        name="attend",
    )(qkv, col, row)


def attend_back_kernel(qkv_ref, p_ref, delta_ref, eb_ref, qsum_ref, vsum_ref):
    width = delta_ref.shape[1]
    low = lax.broadcasted_iota(jnp.int32, (SEG, LANES), 1) < HD

    @pl.when(pl.program_id(0) == 0)
    def _():
        qsum_ref[...] = jnp.zeros_like(qsum_ref)
        vsum_ref[...] = jnp.zeros_like(vsum_ref)

    for pair in range(width // LANES):
        at = pair * LANES
        query = two_heads(qkv_ref[:, at : at + LANES], low)
        key = qkv_ref[:, width + at : width + at + LANES]
        value = qkv_ref[:, 2 * width + at : 2 * width + at + LANES]
        delta = two_heads(delta_ref[:, at : at + LANES], low)
        weight_low = p_ref[0, pair]
        weight = weight_low.astype(F32)
        pressure = against(delta, value)
        moved = weight * (pressure - jnp.sum(weight * pressure, -1, keepdims=True))
        moved = moved.astype(BF16)
        query_delta = product(moved, key)
        query_delta = jnp.where(low, query_delta[:SEG], query_delta[SEG:]) * HD ** (-0.5)
        key_delta = across(moved, query)
        value_delta = across(weight_low, delta)
        eb_ref[:, at : at + LANES] = query_delta.astype(BF16)
        eb_ref[:, width + at : width + at + LANES] = key_delta.astype(BF16)
        eb_ref[:, 2 * width + at : 2 * width + at + LANES] = value_delta.astype(BF16)
        qsum_ref[:, at : at + LANES] += jnp.sum(query_delta, 0, keepdims=True)
        vsum_ref[:, at : at + LANES] += jnp.sum(value_delta, 0, keepdims=True)


def attend_back(qkv, weights, delta):
    rows, width = delta.shape
    segments = rows // SEG
    pairs = width // LANES
    return pl.pallas_call(
        attend_back_kernel,
        grid=(segments,),
        in_specs=[
            pl.BlockSpec((SEG, 3 * width), lambda i: (i, 0)),
            pl.BlockSpec((1, pairs, 2 * SEG, SEG), lambda i: (i, 0, 0, 0)),
            pl.BlockSpec((SEG, width), lambda i: (i, 0)),
        ],
        out_specs=[
            pl.BlockSpec((SEG, 3 * width), lambda i: (i, 0)),
            pl.BlockSpec((1, width), lambda i: (0, 0)),
            pl.BlockSpec((1, width), lambda i: (0, 0)),
        ],
        out_shape=[
            jax.ShapeDtypeStruct((rows, 3 * width), BF16),
            jax.ShapeDtypeStruct((1, width), F32),
            jax.ShapeDtypeStruct((1, width), F32),
        ],
        cost_estimate=pl.CostEstimate(
            flops=16 * rows * SEG * width, bytes_accessed=rows * width * 16, transcendentals=0
        ),
        name="attend_back",
    )(qkv, weights, delta)


def cross(qkv, allowed, batches, width):
    q, k, v = (
        qkv[:, part * width : (part + 1) * width].reshape(batches, -1, H, HD) for part in range(3)
    )
    scores = jnp.einsum("aqhd,akhd->ahqk", q, k, preferred_element_type=F32)
    scores = jnp.where(allowed[:, None], scores, NEGATIVE)
    weight = jnp.exp(scores - jnp.max(scores, -1, keepdims=True))
    weight = weight / jnp.sum(weight, -1, keepdims=True)
    weight_low = weight.astype(BF16)
    mixed = jnp.einsum("ahqk,akhd->aqhd", weight_low, v, preferred_element_type=F32)
    return mixed.reshape(-1, width).astype(BF16), (q, k, v, weight, weight_low)


def cross_back(saved, delta, batches, width):
    q, k, v, weight, weight_low = saved
    delta = delta.reshape(batches, -1, H, HD)
    pressure = jnp.einsum("aqhd,akhd->ahqk", delta, v, preferred_element_type=F32)
    moved = weight * (pressure - jnp.sum(weight * pressure, -1, keepdims=True))
    moved = moved.astype(BF16)
    dq = jnp.einsum("ahqk,akhd->aqhd", moved, k, preferred_element_type=F32)
    dk = jnp.einsum("ahqk,aqhd->akhd", moved, q, preferred_element_type=F32)
    dv = jnp.einsum("ahqk,aqhd->akhd", weight_low, delta, preferred_element_type=F32)
    dq, dk, dv = (part.reshape(-1, width) for part in (dq * HD ** (-0.5), dk, dv))
    return jnp.concatenate([dq, dk, dv], 1).astype(BF16), jnp.sum(dq, 0), jnp.sum(dv, 0)


def forward(start, first, parts, mixer):
    mixing, output, expand, shrink, lift, shift, gain = parts
    width = start.shape[1]
    bias = jnp.concatenate([shift[0], jnp.zeros_like(shift[0]), shift[1]])
    scale = jnp.concatenate([jnp.full((width,), HD ** (-0.5), F32), jnp.ones((2 * width,), F32)])
    qkv = ((product(first, mixing) + bias) * scale).astype(BF16)
    mixed, saved = mixer(qkv)
    unit1, factor1 = unit_of(start + product(mixed, output) + shift[2])
    middle = unit1 * gain[0] + shift[4]
    middle_low = middle.astype(BF16)
    shaped, slope = gelu_parts(product(middle_low, expand) + lift)
    shaped = shaped.astype(BF16)
    slope = slope.astype(BF16)
    unit2, factor2 = unit_of(middle + product(shaped, shrink) + shift[3])
    final = unit2 * gain[1] + shift[5]
    return final, (first, saved, mixed, unit1, factor1, middle_low, shaped, slope, unit2, factor2)


def backward(delta, cache, parts, mixer_back):
    mixing, output, expand, shrink, lift, shift, gain = parts
    first, saved, mixed, unit1, factor1, middle_low, shaped, slope, unit2, factor2 = cache
    e2 = unit_back(delta, gain[1], unit2, factor2)
    gain1, shift5, shift3 = jnp.sum(delta * unit2, 0), jnp.sum(delta, 0), jnp.sum(e2, 0)
    e2b = e2.astype(BF16)
    ez = against(e2b, shrink) * slope.astype(F32)
    lift_grad = jnp.sum(ez, 0)
    ezb = ez.astype(BF16)
    dm = e2 + against(ezb, expand)
    e1 = unit_back(dm, gain[0], unit1, factor1)
    gain0, shift4, shift2 = jnp.sum(dm * unit1, 0), jnp.sum(dm, 0), jnp.sum(e1, 0)
    e1b = e1.astype(BF16)
    eb, shift0, shift1 = mixer_back(saved, against(e1b, output).astype(BF16))
    start_delta = e1 + against(eb, mixing)
    shift_grad = jnp.stack([shift0, shift1, shift2, shift3, shift4, shift5])
    gain_grad = jnp.stack([gain0, gain1])
    factors = ((first, eb), (mixed, e1b), (middle_low, ezb), (shaped, e2b))
    return start_delta, factors, (lift_grad, shift_grad, gain_grad)


def per_device(
    tokens,
    cotangent,
    documents,
    positions,
    inner_mixing,
    inner_output,
    inner_expand,
    inner_shrink,
    inner_lift,
    inner_shifts,
    inner_gains,
    outer_mixing,
    outer_output,
    outer_expand,
    outer_shrink,
    outer_lift,
    outer_shifts,
    outer_gains,
    position_table,
):
    batches = tokens.shape[0]
    width = tokens.shape[3]
    rows = batches * tokens.shape[2]
    own = inner_mixing.shape[0]
    hidden = inner_expand.shape[1]
    ratio = hidden // width
    seqs = lax.axis_size("seq")
    toks = lax.axis_size("tok")
    slots = tokens.shape[2] // SEG
    places = position_table.shape[0]
    tok = lax.axis_index("tok")

    def folded(part):
        return jnp.concatenate([part[j * own : (j + 1) * own] for j in range(ratio)], 1)

    def unfolded(part):
        return (
            part.reshape(-1, own, ratio, width).transpose(0, 2, 1, 3).reshape(ratio * width, width)
        )

    small = [
        inner_lift.reshape(own, ratio),
        inner_shifts.T,
        inner_gains.T,
        outer_lift.reshape(own, ratio),
        outer_shifts.T,
        outer_gains.T,
        position_table.T,
    ]
    count = sum(part.shape[1] for part in small)
    small.append(jnp.zeros((own, -count % LANES), BF16))

    lead = lax.all_gather(
        jnp.concatenate([inner_mixing] + small, 1), ALL, axis=0, tiled=True
    )
    rest = lax.all_gather(
        jnp.concatenate([inner_output, inner_expand, folded(inner_shrink)], 1),
        ALL,
        axis=0,
        tiled=True,
    )
    outer_all = lax.all_gather(
        jnp.concatenate([outer_mixing, outer_output, outer_expand, folded(outer_shrink)], 1),
        ALL,
        axis=0,
        tiled=True,
    )
    summary_cotangent = cotangent.reshape(batches, slots, SEG, width)[:, :, 0]
    summary_docs = documents.reshape(batches, slots, SEG)[:, :, :1]
    early = jnp.concatenate(
        [summary_cotangent, jnp.broadcast_to(summary_docs.astype(BF16), (batches, slots, LANES))], 2
    )
    early = lax.all_gather(early, "tok", axis=1, tiled=True)

    small_all = lead[:, 3 * width :].astype(F32)
    at = 0

    def take(columns):
        nonlocal at
        at += columns
        return small_all[:, at - columns : at]

    inner_small = (take(ratio).reshape(hidden), take(6).T, take(2).T)
    outer_small = (take(ratio).reshape(hidden), take(6).T, take(2).T)
    table = lead[:, 3 * width + at : 3 * width + at + places].T
    inner = (
        lead[:, : 3 * width],
        rest[:, :width],
        rest[:, width : width + hidden],
        unfolded(rest[:, width + hidden :]),
    ) + inner_small
    outer = (
        outer_all[:, : 3 * width],
        outer_all[:, 3 * width : 4 * width],
        outer_all[:, 4 * width : 4 * width + hidden],
        unfolded(outer_all[:, 4 * width + hidden :]),
    ) + outer_small

    first = tokens.reshape(rows, width)
    docs = documents.reshape(rows)
    col = docs[:, None]
    row = docs.reshape(-1, 1, SEG)

    def within(qkv):
        mixed, weights = attend(qkv, col, row, width)
        return mixed, (qkv, weights)

    def within_back(saved, delta):
        eb, qsum, vsum = attend_back(saved[0], saved[1], delta)
        return eb, qsum[0], vsum[0]

    h1, cache = forward(first.astype(F32), first, inner, within)
    grouped = h1.reshape(batches, slots, SEG, width)

    picked = (positions.reshape(-1, 1) == jnp.arange(places, dtype=jnp.int32)[None, :]).astype(BF16)
    c_own = grouped[:, :, 0] + product(picked, table).reshape(batches, slots, width)
    c_all = lax.all_gather(
        jnp.concatenate([c_own, picked.astype(F32).reshape(batches, slots, places)], 2)
        if places % LANES == 0
        else jnp.concatenate(
            [
                c_own,
                jnp.pad(
                    picked.astype(F32).reshape(batches, slots, places),
                    ((0, 0), (0, 0), (0, -places % LANES)),
                ),
            ],
            2,
        ),
        "tok",
        axis=1,
        tiled=True,
    )
    count = c_all.shape[1]
    picked_all = c_all[:, :, width : width + places].reshape(batches * count, places)
    c = c_all[:, :, :width].reshape(batches * count, width)
    docs_all = early[:, :, width]
    allowed = docs_all[:, :, None] == docs_all[:, None, :]
    c2, outer_cache = forward(
        c, c.astype(BF16), outer, lambda qkv: cross(qkv, allowed, batches, width)
    )
    dc, outer_factors, outer_sums = backward(
        early[:, :, :width].reshape(batches * count, width).astype(F32),
        outer_cache,
        outer,
        lambda saved, delta: cross_back(saved, delta, batches, width),
    )

    def mine(value):
        parts = value.reshape(value.shape[0], seqs, toks, -1)
        return lax.dynamic_index_in_dim(parts, tok, 2, keepdims=False)

    pieces = []
    for left, right in outer_factors:
        left = mine(left)
        piece = across(left.reshape(left.shape[0], -1), right)
        if left.shape[2] != own:
            piece = piece.reshape(seqs, ratio, own, width).transpose(0, 2, 1, 3)
        pieces.append(piece.reshape(seqs, own, -1))
    table_grad = lax.dot_general(
        picked_all, dc, (((0,), (0,)), ((), ())), precision=lax.Precision.HIGHEST
    )
    lift_grad, shift_grad, gain_grad = outer_sums
    sums = [mine(lift_grad[None]).reshape(seqs, own, ratio)]
    for part in (shift_grad, gain_grad, table_grad):
        sums.append(mine(part).transpose(1, 2, 0))
    sums = jnp.concatenate(sums, 2)
    sums = jnp.pad(sums, ((0, 0), (0, 0), (0, -sums.shape[2] % LANES)))
    outer_total = jnp.concatenate(pieces + [sums], 2).astype(BF16)
    outer_total = lax.psum_scatter(outer_total, "seq", scatter_dimension=0, tiled=False)

    def own_rows(value):
        return lax.dynamic_slice_in_dim(
            value.reshape(batches, count, width), tok * slots, slots, axis=1
        )

    output = (
        jnp.concatenate([own_rows(c2)[:, :, None], grouped[:, :, 1:]], 2)
        .astype(BF16)
        .reshape(tokens.shape)
    )
    incoming = cotangent.astype(F32).reshape(batches, slots, SEG, width)
    delta = jnp.concatenate([own_rows(dc)[:, :, None], incoming[:, :, 1:]], 2).reshape(rows, width)
    dx, factors, sums = backward(delta, cache, inner, within_back)
    tokens_gradient = dx.astype(BF16).reshape(tokens.shape)
    mixing_grad, output_grad, expand_grad, shrink_grad = (
        across(left, right).astype(BF16) for left, right in factors
    )
    lift_grad, shift_grad, gain_grad = sums
    sums = jnp.concatenate([lift_grad.reshape(width, ratio), shift_grad.T, gain_grad.T], 1)
    sums = jnp.pad(sums, ((0, 0), (0, -sums.shape[1] % LANES))).astype(BF16)
    shrink_own = lax.psum_scatter(shrink_grad, ALL, scatter_dimension=0, tiled=True)
    expand_own = lax.psum_scatter(expand_grad, ALL, scatter_dimension=0, tiled=True)
    mixing_own = lax.psum_scatter(mixing_grad, ALL, scatter_dimension=0, tiled=True)
    last = lax.psum_scatter(
        jnp.concatenate([output_grad, sums], 1), ALL, scatter_dimension=0, tiled=True
    )

    def vectors(part):
        return (
            part[:, :ratio].reshape(-1),
            part[:, ratio : ratio + 6].T,
            part[:, ratio + 6 : ratio + 8].T,
        )

    last = last.astype(F32)
    outer_total = outer_total.astype(F32)
    outer_shrink_own = outer_total[:, 4 * width + hidden : 4 * width + 2 * hidden]
    outer_shrink_own = (
        outer_shrink_own.reshape(own, ratio, width).transpose(1, 0, 2).reshape(ratio * own, width)
    )
    outer_sums = outer_total[:, 4 * width + 2 * hidden :]
    return (
        (
            output,
            tokens_gradient,
            mixing_own.astype(F32),
            last[:, :width],
            expand_own.astype(F32),
            shrink_own.astype(F32),
        )
        + vectors(last[:, width:])
        + (
            outer_total[:, : 3 * width],
            outer_total[:, 3 * width : 4 * width],
            outer_total[:, 4 * width : 4 * width + hidden],
            outer_shrink_own,
        )
        + vectors(outer_sums)
        + (outer_sums[:, ratio + 8 : ratio + 8 + places].T,)
    )


ROWS = P(None, "seq", "tok", None)
IDS = P(None, "seq", "tok")
TALL = P(ALL, None)
FLAT = P(ALL)
WIDE = P(None, ALL)
LAYER = (TALL, TALL, TALL, TALL, FLAT, WIDE, WIDE)


def solution(mesh):
    return jax.shard_map(
        per_device,
        mesh=mesh,
        in_specs=(ROWS, ROWS, IDS, IDS) + LAYER + LAYER + (WIDE,),
        out_specs=(ROWS, ROWS) + LAYER + LAYER + (WIDE,),
        check_vma=False,
    )
```

time: 2140 us -> 1000 us (0.47)
  waiting for transfers between devices: 1090 us -> 573 us
  blocking collectives: 350 us -> 19.9 us
  matrix products: 351 us -> 156 us
  local copies, waits for them, and re-layouts: 268 us -> 163 us
  Pallas kernels: 0 us -> 28.9 us
    reduce_scatter x7 -> x2, waiting for transfers between devices: 899 us -> 220 us  [the longest x1 111 us: per_device(): lax.psum_scatter(expand_grad, ALL, scatter_dimension=0, tiled=True)]
    all_gather x14 -> x2, blocking collectives: 284 us -> 19.9 us  [the longest x1 10.7 us: per_device(): early = lax.all_gather(early, 'tok', axis=1, tiled=True)]
    all_gather x8 -> x3, waiting for transfers between devices: 0.07 us -> 144 us  [the longest x1 62.8 us: per_device(): lax.all_gather(jnp.concatenate([inner_output, inner_expand, folded(inner_...]
    dot_general x88 -> x16, matrix products: 171 us -> 51.6 us  [the longest x9 40.3 us: product(): return jnp.dot(left, right, preferred_element_type=F32)]
    another operation x96 -> x21, local copies, waits for them, and re-layouts: 120 us -> 23 us  [the longest x11 12 us: backward(): shift_grad = jnp.stack([shift0, shift1, shift2, shift3, shift4, shift5])]
    dot_general x32 -> x8, matrix products: 118 us -> 40.1 us  [across(): lax.dot_general(left, right, (((0,), (0,)), ((), ())), preferred_element_...]
    unnamed x2 -> x0, blocking collectives: 66.2 us -> none
    pallas_call x0 -> x2, Pallas kernels: none -> 28.9 us  [the longest x1 18.3 us: attend_back(): pl.pallas_call(attend_back_kernel, grid=(segments,), in_specs=[pl.BlockSp...]
  transfers between devices with their start and end apart: 18 -> 8, of which waited for: 9 -> 8; matrix products, arithmetic and copies ran while one was open for 16% -> 15% of each run, Pallas kernels for 0% -> 1%
where the time goes in v1:
time: 1000 us; the launch traced here: 992 us
  waiting for transfers between devices  573 us (57%)
  local copies, waits for them, and re-layouts  163 us (16%)
  matrix products  156 us (16%)
  other arithmetic  36 us (4%)
  Pallas kernels  28.9 us (3%)
  blocking collectives  19.9 us (2%)
  between operations  15.4 us (2%)
    unnamed x11, waiting for transfers between devices  209 us
    reduce_scatter x1, waiting for transfers between devices, per_device(): lax.psum_scatter(expand_grad, ALL, scatter_dimension=0, tiled=True)  111 us
    reduce_scatter x1, waiting for transfers between devices, per_device(): lax.psum_scatter(shrink_grad, ALL, scatter_dimension=0, tiled=True)  109 us
    dot_general x8, matrix products, against(): lax.dot_general(left, right, (((1,), (1,)), ((), ())), preferred_element_...  63.8 us
    all_gather x1, waiting for transfers between devices, per_device(): lax.all_gather(jnp.concatenate([inner_output, inner_expand, folded(inner_...  62.8 us
    all_gather x1, waiting for transfers between devices, per_device(): lax.all_gather(jnp.concatenate([outer_mixing, outer_output, outer_expand,...  48.9 us
    dot_general x9, matrix products, product(): return jnp.dot(left, right, preferred_element_type=F32)  40.3 us
    dot_general x8, matrix products, across(): lax.dot_general(left, right, (((0,), (0,)), ((), ())), preferred_element_...  40.1 us
  transfers between devices with their start and end apart: 8, of which 8 were waited for; matrix products, arithmetic and copies ran while one was open for 15% of the time, Pallas kernels for 1%

profile of v1, /device:TPU:0, one launch (start us, length us, event | category | flops | bytes accessed | tf_op | source)
XLA Modules:
  0.0 992.1 jit_solution(937322875471500862)
XLA Ops:
  28.5 10.7 %all_gather.19 = bf16[4,16,896]{2,0,1:T(4,128)(2,1)S(1)} all-gather(bf16[4,2,896]{2,0,1:T(4,128)(2,1)S(1)} %pad_maximum_fusion.6), channel_id=1, replica_groups=mesh['seq'=4,'tok'=8] {'tok'}, dimensions={1}, use_global_device_ids=true | all-gather | bytes 129024 | tf_op jit(solution)/shard_map/all_gather | solution.py:302
  44.4 32.8 %all-gather.4.cloned.1.call-done = bf16[768,2432]{1,0:T(8,128)(2,1)} async-done(((bf16[24,2432]{1,0:T(8,128)(2,1)}), bf16[768,2432]{1,0:T(8,128)(2,1)}) %all-gather.4.cloned.1.call-update) | async-done | bytes 3735568 | tf_op jit(solution)/shard_map/all_gather | solution.py:282
  86.8 5.9 fusion.8.qkv_ref
  92.7 10.6 %attend.1 = (bf16[1024,768]{1,0:T(8,128)(2,1)}, bf16[8,6,256,128]{3,2,1,0:T(8,128)(2,1)}) custom-call(bf16[1024,2304]{1,0:T(8,128)(2,1)} %fusion.8.qkv_ref, s32[1024,1]{1,0:T(8,128)} %copy.389.col_ref, s32[8,1,128]{2,1,0:T(1,128)} %bitcast.214), custom_call_target="tpu_custom_call" | custom-call | flops 805306368 | bytes 7864320 | tf_op jit(solution)/shard_map/attend/pallas_call | solution.py:81
  103.3 62.8 %all-gather.6.cloned.1.call-done = bf16[768,6912]{1,0:T(8,128)(2,1)} async-done(((bf16[24,6912]{1,0:T(8,128)(2,1)}), bf16[768,6912]{1,0:T(8,128)(2,1)}) %all-gather.6.cloned.1.call-update) | async-done | bytes 10616848 | tf_op jit(solution)/shard_map/all_gather | solution.py:285
  170.9 9.8 reshape.351
  188.5 11.7 %multiply_convert_fusion = (bf16[1024,3072]{1,0:T(8,128)(2,1)S(1)}, f32[1024,3072]{1,0:T(8,128)}) fusion(f32[3072]{0:T(1024)S(1)} %add.240, bf16[768,6912]{1,0:T(8,128)(2,1)} %all-gather.6.cloned.1.call-done, f32[1024,768]{1,0:T(8,128)S(1)} %get-tuple-element.225, f32[768]{0:T(1024)S(1)} %get-tuple-element.185, f32[768]{0:T(1024)S(1)} %get-tuple-element.247, ...), kind=kOutput, calls=%fused_computation.8 | convolution fusion | flops 4854644736 | bytes 26765312 | tf_op jit(solution)/shard_map/dot_general | solution.py:23
  208.4 9.2 all_gather.17
  221.9 48.9 %all-gather.8.cloned.1.call-done = bf16[768,9216]{1,0:T(8,128)(2,1)} async-done(((bf16[24,9216]{1,0:T(8,128)(2,1)}), bf16[768,9216]{1,0:T(8,128)(2,1)}) %all-gather.8.cloned.1.call-update) | async-done | bytes 14155792 | tf_op jit(solution)/shard_map/all_gather | solution.py:291
  291.2 9.9 reshape.361
  301.1 5.6 copy.403
  401.6 21.2 %fusion.6 = (bf16[3072]{0:T(1024)(128)(2,1)}, bf16[1024,3072]{1,0:T(8,128)(2,1)}, f32[1024,3072]{1,0:T(8,128)}) fusion(f32[1024,3072]{1,0:T(8,128)} %get-tuple-element.227, f32[3072]{0:T(1024)} %copy-done.45, bf16[3072,768]{1,0:T(8,128)(2,1)} %bitcast.196, f32[1024,768]{1,0:T(8,128)} %get-tuple-element.202), kind=kOutput, calls=%fused_computation.11 | convolution fusion | flops 4873516032 | bytes 39340032 | tf_op jit(solution)/shard_map/dot_general | solution.py:31
  422.9 16.0 %multiply_reduce_fusion = (bf16[768]{0:T(1024)(128)(2,1)S(1)}, f32[1024]{0:T(1024)S(1)}, f32[1024]{0:T(1024)S(1)}, bf16[768]{0:T(1024)(128)(2,1)S(1)}, f32[1024,768]{1,0:T(8,128)}) fusion(f32[1024,768]{1,0:T(8,128)S(1)} %copy-done.2, f32[1024]{0:T(1024)S(1)} %copy-done.41, f32[1024]{0:T(1024)S(1)} %copy-done.35, f32[768]{0:T(1024)S(1)} %copy-done.39, ...), kind=kOutput, calls=%fused_computation.40 | convolution fusion | flops 4849135616 | bytes 33052672 | tf_op jit(solution)/shard_map/dot_general | solution.py:31
  450.0 18.3 %attend_back.1 = (bf16[1024,2304]{1,0:T(8,128)(2,1)}, f32[1,768]{1,0:T(1,128)}, f32[1,768]{1,0:T(1,128)}) custom-call(bf16[1024,2304]{1,0:T(8,128)(2,1)} %fusion.8.qkv_ref, bf16[8,6,256,128]{3,2,1,0:T(8,128)(2,1)} %get-tuple-element.23.p_ref, bf16[1024,768]{1,0:T(8,128)(2,1)} %convolution_convert_fusion.5.delta_ref), custom_call_target="tpu_custom_call" | custom-call | flops 1610612736 | bytes 12582912 | tf_op jit(solution)/shard_map/attend_back/pallas_call | solution.py:139
  488.7 8.5 fusion.9
  497.3 5.8 copy.444
  503.2 9.7 convolution_convert_fusion
  513.5 14.2 %convolution_convert_fusion.1 = bf16[768,3072]{1,0:T(8,128)(2,1)} fusion(f32[1024,3072]{1,0:T(8,128)} %get-tuple-element.243, bf16[1024,3072]{1,0:T(8,128)(2,1)} %get-tuple-element.198, f32[1024,768]{1,0:T(8,128)S(1)} %copy-done.2, f32[768]{0:T(1024)S(1)} %copy-done.55, f32[768]{0:T(1024)S(1)} %copy-done.39, f32[1024]{0:T(1024)S(1)} %copy-done.41, ...), kind=kOutput, calls=%fused_computation.14 | convolution fusion | flops 4847566848 | bytes 26753024 | tf_op jit(solution)/shard_map/dot_general | solution.py:27
  531.7 8.5 add_convert_fusion
  540.2 70.5 %all-reduce.7.cloned.1.call-done = bf16[768,896]{0,1:T(8,128)(2,1)} async-done(((bf16[768,896]{0,1:T(8,128)(2,1)}), bf16[768,896]{0,1:T(8,128)(2,1)}) %all-reduce.7.cloned.1.call-update) | async-done | bytes 1376272
  614.5 36.9 %reduce-scatter.16.cloned.1.call-done = bf16[1,24,9344]{2,1,0:T(8,128)(2,1)} async-done(((bf16[4,24,9344]{2,1,0:T(8,128)(2,1)}), bf16[1,24,9344]{2,1,0:T(8,128)(2,1)}) %reduce-scatter.16.cloned.1.call-update) | async-done | bytes 448528
  658.3 101.1 %reduce-scatter.14.cloned.1.call-done = bf16[24,2304]{1,0:T(8,128)(2,1)} async-done(((bf16[768,2304]{1,0:T(8,128)(2,1)}), bf16[24,2304]{1,0:T(8,128)(2,1)}) %reduce-scatter.14.cloned.1.call-update) | async-done | bytes 110608
  761.6 109.3 %reduce-scatter.12.cloned.1.call-done = bf16[96,768]{1,0:T(8,128)(2,1)} async-done(((bf16[3072,768]{1,0:T(8,128)(2,1)}), bf16[96,768]{1,0:T(8,128)(2,1)}) %reduce-scatter.12.cloned.1.call-update) | async-done | bytes 147472 | tf_op jit(solution)/shard_map/reduce_scatter | solution.py:421
  872.5 110.9 %reduce-scatter.10.cloned.1.call-done = bf16[24,3072]{1,0:T(8,128)(2,1)} async-done(((bf16[768,3072]{1,0:T(8,128)(2,1)}), bf16[24,3072]{1,0:T(8,128)(2,1)}) %reduce-scatter.10.cloned.1.call-update) | async-done | bytes 147472 | tf_op jit(solution)/shard_map/reduce_scatter | solution.py:422
  (367 shorter events, 227.9 us)
Async XLA Ops:
  7.2 33.9 %copy-start.56 = (s32[4,1,2]{0,2,1:T(2,128)S(1)}, s32[4,1,2]{0,2,1:T(2,128)}, u32[]{:S(2)}) copy-start(s32[4,1,2]{0,2,1:T(2,128)} %param.22) | copy-start | bytes 100
  7.2 32.9 %copy-start.37 = (s32[4,1,256]{2,1,0:T(1,128)S(1)}, s32[4,1,256]{2,1,0:T(1,128)}, u32[]{:S(2)}) copy-start(s32[4,1,256]{2,1,0:T(1,128)} %param.21) | copy-start | bytes 12292
  7.2 34.0 %copy-start.5 = (bf16[4,1,256,768]{3,2,1,0:T(8,128)(2,1)S(1)}, bf16[4,1,256,768]{3,2,1,0:T(8,128)(2,1)}, u32[]{:S(2)}) copy-start(bf16[4,1,256,768]{3,2,1,0:T(8,128)(2,1)} %param.20) | copy-start | bytes 4718596
  7.2 69.9 %all-gather.4.cloned.1.call-start = ((), (), s32[]{:S(2)}) async-start(), calls=%async_computation.4 | async-start | bytes 3852288 | tf_op jit(solution)/shard_map/all_gather | solution.py:282
  13.6 152.5 %all-gather.6.cloned.1.call-start = ((), (), s32[]{:S(2)}) async-start(), calls=%async_computation.5 | async-start | bytes 10948608 | tf_op jit(solution)/shard_map/all_gather | solution.py:285
  19.2 251.5 %all-gather.8.cloned.1.call-start = ((), (), s32[]{:S(2)}) async-start(), calls=%async_computation.6 | async-start | bytes 14598144 | tf_op jit(solution)/shard_map/all_gather | solution.py:291
  25.7 585.0 %all-reduce.7.cloned.1.call-start = ((), (), s32[]{:S(2)}) async-start(), calls=%async_computation.10 | async-start | bytes 2752512
  80.5 107.9 %copy-start.45 = (f32[3072]{0:T(1024)}, f32[3072]{0:T(1024)S(1)}, u32[]{:S(2)}) copy-start(f32[3072]{0:T(1024)S(1)} %add.240) | copy-start | bytes 36868
  86.7 113.4 %copy-start.38 = (f32[768]{0:T(1024)}, f32[768]{0:T(1024)S(1)}, u32[]{:S(2)}) copy-start(f32[768]{0:T(1024)S(1)} %get-tuple-element.247) | copy-start | bytes 9220
  86.7 113.4 %copy-start.54 = (f32[768]{0:T(1024)}, f32[768]{0:T(1024)S(1)}, u32[]{:S(2)}) copy-start(f32[768]{0:T(1024)S(1)} %get-tuple-element.185) | copy-start | bytes 9220
  184.1 16.1 %copy-start.6 = (bf16[32,4,24,768]{3,2,1,0:T(8,128)(2,1)}, bf16[32,4,24,768]{3,2,1,0:T(8,128)(2,1)S(1)}, u32[]{:S(2)}) copy-start(bf16[32,4,24,768]{3,2,1,0:T(8,128)(2,1)S(1)} %copy.390) | copy-start | bytes 14155780
  187.9 12.3 %copy-start.1 = (f32[1024,768]{1,0:T(8,128)}, f32[1024,768]{1,0:T(8,128)S(1)}, u32[]{:S(2)}) copy-start(f32[1024,768]{1,0:T(8,128)S(1)} %get-tuple-element.225) | copy-start | bytes 9437188
  187.9 12.3 %copy-start.34 = (f32[1024]{0:T(1024)}, f32[1024]{0:T(1024)S(1)}, u32[]{:S(2)}) copy-start(f32[1024]{0:T(1024)S(1)} %broadcast_multiply_fusion.6) | copy-start | bytes 12292
  206.2 64.6 %copy-start.62 = (f32[2304]{0:T(1024)S(1)}, f32[2304]{0:T(1024)}, u32[]{:S(2)}) copy-start(f32[2304]{0:T(1024)} %constant.76.clone.1) | copy-start | bytes 27652
  218.4 55.8 %copy-start.11 = (f32[4,16,768]{2,1,0:T(8,128)}, f32[4,16,768]{2,1,0:T(8,128)S(1)}, u32[]{:S(2)}) copy-start(f32[4,16,768]{2,1,0:T(8,128)S(1)} %copy.394) | copy-start | bytes 589828
  339.0 48.0 %copy-start.15 = (f32[64,768]{1,0:T(8,128)S(1)}, f32[64,768]{1,0:T(8,128)}, u32[]{:S(2)}) copy-start(f32[64,768]{1,0:T(8,128)} %copy-done.14) | copy-start | bytes 589828
  401.6 21.2 %copy-start.2 = (f32[1024,768]{1,0:T(8,128)S(1)}, f32[1024,768]{1,0:T(8,128)}, u32[]{:S(2)}) copy-start(f32[1024,768]{1,0:T(8,128)} %copy-done.1) | copy-start | bytes 9437188
  401.6 21.2 %copy-start.35 = (f32[1024]{0:T(1024)S(1)}, f32[1024]{0:T(1024)}, u32[]{:S(2)}) copy-start(f32[1024]{0:T(1024)} %copy-done.34) | copy-start | bytes 12292
  401.6 21.2 %copy-start.39 = (f32[768]{0:T(1024)S(1)}, f32[768]{0:T(1024)}, u32[]{:S(2)}) copy-start(f32[768]{0:T(1024)} %copy-done.38) | copy-start | bytes 9220
  401.6 21.2 %copy-start.41 = (f32[1024]{0:T(1024)S(1)}, f32[1024]{0:T(1024)}, u32[]{:S(2)}) copy-start(f32[1024]{0:T(1024)} %copy-done.40) | copy-start | bytes 12292
  481.4 170.1 %reduce-scatter.16.cloned.1.call-start = ((), (), s32[]{:S(2)}) async-start(), calls=%async_computation.11 | async-start | bytes 2242560
  488.7 270.7 %reduce-scatter.14.cloned.1.call-start = ((), (), s32[]{:S(2)}) async-start(), calls=%async_computation.9 | async-start | bytes 3649536
  503.1 367.7 %reduce-scatter.12.cloned.1.call-start = ((), (), s32[]{:S(2)}) async-start(), calls=%async_computation.8 | async-start | bytes 4866048 | tf_op jit(solution)/shard_map/reduce_scatter | solution.py:421
  512.9 470.5 %reduce-scatter.10.cloned.1.call-start = ((), (), s32[]{:S(2)}) async-start(), calls=%async_computation.7 | async-start | bytes 4866048 | tf_op jit(solution)/shard_map/reduce_scatter | solution.py:422
  (48 other events, 195.7 us)
Sparse Core Ops, SparseCore 0:
  13.7 63.3 all-gather.3
  80.0 86.0 all-gather.5
  169.0 101.7 all-gather.7
  481.5 129.1 all-reduce.6
  612.9 38.5 reduce-scatter.15
  656.7 102.6 reduce-scatter.13
  764.9 105.9 reduce-scatter.11
  877.2 106.1 reduce-scatter.9
